TPU v7x, 32 devices: a whole 2x2x4 slice. The times are simulated.
32 devices in a mesh: dp: 4 (over y, x), mp: 8 (over z, core).
Axes of the slice: x: 2, y: 2, z: 4, core: 2. Of those that a mesh axis runs over, the one named last changes fastest.
Arguments:
- fields: float32 [4, 2048, 192], P('dp', 'mp'), may hold values from -6 to 6
- targets: float32 [4, 2, 2048, 192], P('dp', None, 'mp'), may hold values from -6 to 6
- land_mask: int32 [4, 2048, 4], P('dp', 'mp'), may hold values 0 or 1
- lead_index: int32 [4, 2], P('dp'), may hold values from 0 to 6
- var_ids: int32 [48], replicated, may hold values from 0 to 47, each once
- tables: float32 [440, 1024], replicated, may hold values from -4 to 4
- norm_gains: float32 [6, 1024], replicated, may hold values from -0.5 to 1.4, as said below
- tables_first: float32 [440, 1024], replicated, may hold values from -9.536743e-06 to 9.536743e-06
- tables_second: float32 [440, 1024], replicated, may hold values from 9.586172e-14 to 1.5337875e-12
- gains_first: float32 [6, 1024], replicated, may hold values from -3.8146973e-05 to 3.8146973e-05
- gains_second: float32 [6, 1024], replicated, may hold values from 1.5337875e-12 to 2.45406e-11
- w_qkv: float32 [1024, 3072], P(None, 'mp'), may hold values from -0.1875 to 0.1875
- qkv_first: float32 [1024, 3072], P('dp', 'mp'), may hold values from -9.536743e-06 to 9.536743e-06
- qkv_second: float32 [1024, 3072], P('dp', 'mp'), may hold values from 9.586172e-14 to 1.5337875e-12
- w_out: float32 [1024, 1024], P('mp'), may hold values from -0.5 to 0.5
- out_first: float32 [1024, 1024], P('mp', 'dp'), may hold values from -9.536743e-06 to 9.536743e-06
- out_second: float32 [1024, 1024], P('mp', 'dp'), may hold values from 9.586172e-14 to 1.5337875e-12
- w_up: float32 [1024, 4096], P(None, 'mp'), may hold values from -0.1875 to 0.1875
- up_first: float32 [1024, 4096], P('dp', 'mp'), may hold values from -9.536743e-06 to 9.536743e-06
- up_second: float32 [1024, 4096], P('dp', 'mp'), may hold values from 9.586172e-14 to 1.5337875e-12
- w_down: float32 [4096, 1024], P('mp'), may hold values from -0.09375 to 0.09375
- down_first: float32 [4096, 1024], P('mp', 'dp'), may hold values from -9.536743e-06 to 9.536743e-06
- down_second: float32 [4096, 1024], P('mp', 'dp'), may hold values from 9.586172e-14 to 1.5337875e-12
- qkv_average: float32 [1024, 3072], P('dp', 'mp'), may hold values from -0.1875 to 0.1875
Outputs:
- loss: float32 [], replicated
- grad_norm: float32 [], replicated
- tables_new: float32 [440, 1024], replicated
- tables_first_new: float32 [440, 1024], replicated
- tables_second_new: float32 [440, 1024], replicated
- gains_new: float32 [6, 1024], replicated
- gains_first_new: float32 [6, 1024], replicated
- gains_second_new: float32 [6, 1024], replicated
- qkv_new: float32 [1024, 3072], P('dp', 'mp')
- qkv_first_new: float32 [1024, 3072], P('dp', 'mp')
- qkv_second_new: float32 [1024, 3072], P('dp', 'mp')
- out_new: float32 [1024, 1024], P('mp', 'dp')
- out_first_new: float32 [1024, 1024], P('mp', 'dp')
- out_second_new: float32 [1024, 1024], P('mp', 'dp')
- up_new: float32 [1024, 4096], P('dp', 'mp')
- up_first_new: float32 [1024, 4096], P('dp', 'mp')
- up_second_new: float32 [1024, 4096], P('dp', 'mp')
- down_new: float32 [4096, 1024], P('mp', 'dp')
- down_first_new: float32 [4096, 1024], P('mp', 'dp')
- down_second_new: float32 [4096, 1024], P('mp', 'dp')
- qkv_average_new: float32 [1024, 3072], P('dp', 'mp')
Inputs may be any that keep to these rules, and one draw needn't show every extreme that they name: `var_ids`: each value once. `norm_gains`: even rows gains, odd rows biases.
All inputs are finite; a program needn't handle non-finite values. No bound on the sum of `land_mask` on one device may be relied on, other than what follows from the above.
Results may differ from a plain program's by a relative error of at most 0.0054.
The roundings to bfloat16 on the way count: a program that leaves them out, or rounds other values in their place, can miss the bound.
Values may be sent and summed in bfloat16 or wider, within the bound.
A program may use at most 256 MiB of HBM per device.

v0:
```python
from functools import partial
import math
import jax
import jax.numpy as jnp
from jax import lax
from jax.sharding import PartitionSpec as P

D = 1024
HEADS = 16
HEAD_DIM = 64
V = 48
PATCH_ROWS = 32
PATCH_COLS = 64
LEADS = 7
QBLOCK = 512
highest = lax.Precision.HIGHEST
eps_norm = 1e-05
clip_norm = 0.05
beta_first = 0.9
beta_second = 0.999
adam_eps = 1e-08
decay_rate = 0.1
lr_matrix = 0.04
lr_table = 0.1
lr_gain = 0.3
average_keep = 0.9
first_fix = 1.0 - 0.9**10
second_fix = 1.0 - 0.999**10


def layer_norm(values, gain, bias):
    center = values - jnp.mean(values, axis=-1, keepdims=True)
    spread = jnp.mean(center * center, axis=-1, keepdims=True)
    return center * lax.rsqrt(spread + eps_norm) * gain + bias


def lat_weights(pixel_rows):
    row_index = jnp.arange(pixel_rows, dtype=jnp.float32)
    cosine = jnp.cos(((row_index + 0.5) / pixel_rows - 0.5) * math.pi)
    return cosine / jnp.mean(cosine)


def embed_tokens(cells, tables, var_hot, lead_hot):
    count_rows = cells.shape[0]
    patch_tab = tables[: 4 * V].reshape(V, 4, HEADS, HEAD_DIM)
    var_tab = jnp.dot(var_hot, tables[4 * V : 5 * V], precision=highest).reshape(V, HEADS, HEAD_DIM)
    lead_vec = jnp.dot(lead_hot, tables[5 * V : 5 * V + LEADS], precision=highest)
    query = tables[5 * V + LEADS].reshape(HEADS, HEAD_DIM)
    keyed = jnp.einsum("vphc,hc->vph", patch_tab, query, precision=highest)
    biased = jnp.einsum("vhc,hc->vh", var_tab, query, precision=highest)
    pixels = cells.reshape(count_rows, V, 4)
    scores = (jnp.einsum("tvp,vph->tvh", pixels, keyed, precision=highest) + biased) * HEAD_DIM ** (
        -0.5
    )
    shares = jax.nn.softmax(scores, axis=1)
    mixed = (shares[:, :, None, :] * pixels[:, :, :, None]).reshape(count_rows, 4 * V, HEADS)
    merged = jnp.einsum(
        "tkh,khc->thc", mixed, patch_tab.reshape(4 * V, HEADS, HEAD_DIM), precision=highest
    )
    merged = merged + jnp.einsum("tvh,vhc->thc", shares, var_tab, precision=highest)
    return merged.reshape(count_rows, D) + lead_vec


def predict(last_rows, gain, bias, tables):
    normed = layer_norm(last_rows, gain, bias)
    return lax.dot_general(
        normed, tables[5 * V + LEADS + 1 :], (((1,), (1,)), ((), ())), precision=highest
    )


def product_nn(left, right):
    return jnp.dot(left, right, preferred_element_type=jnp.float32)


def product_tn(left, right):
    return lax.dot_general(
        left, right, (((0,), (0,)), ((), ())), preferred_element_type=jnp.float32
    )


def product_nt(left, right):
    return lax.dot_general(
        left, right, (((1,), (1,)), ((), ())), preferred_element_type=jnp.float32
    )


def spread_rows(normed):
    return lax.all_gather(normed, "mp", axis=0, tiled=True)


def fold_rows(partial_sum):
    return lax.psum_scatter(
        partial_sum.astype(jnp.bfloat16), "mp", scatter_dimension=0, tiled=True
    ).astype(jnp.float32)


def spread_grads(grad_rows):
    return lax.all_gather(grad_rows, "mp", axis=0, tiled=True)


def fold_grads(partial_sum):
    return lax.psum_scatter(
        partial_sum.astype(jnp.bfloat16), "mp", scatter_dimension=0, tiled=True
    ).astype(jnp.float32)


def attend(queries, keys, values):
    total, heads, width = queries.shape
    blocks = queries.reshape(total // QBLOCK, QBLOCK, heads, width)

    def one_block(block):
        scores = jnp.einsum(
            "qhc,khc->hqk", block, keys, preferred_element_type=jnp.float32
        ) * width ** (-0.5)
        largest = jnp.max(scores, axis=-1, keepdims=True)
        raised = jnp.exp(scores - largest)
        totals = jnp.sum(raised, axis=-1, keepdims=True)
        probs = (raised / totals).astype(jnp.bfloat16)
        result = jnp.einsum("hqk,khc->qhc", probs, values, preferred_element_type=jnp.float32)
        return (result.astype(jnp.bfloat16), (largest + jnp.log(totals))[..., 0])

    results, logsum = lax.map(one_block, blocks)
    return (results.reshape(total, heads * width), logsum)


def attend_back(grad_out, queries, keys, values, logsum):
    total, heads, width = queries.shape
    scale = width ** (-0.5)
    blocks = queries.reshape(total // QBLOCK, QBLOCK, heads, width)
    grad_blocks = grad_out.reshape(total // QBLOCK, QBLOCK, heads, width)

    def one_block(carry, item):
        key_grad, value_grad = carry
        block, block_grad, block_lse = item
        scores = jnp.einsum("qhc,khc->hqk", block, keys, preferred_element_type=jnp.float32) * scale
        probs = jnp.exp(scores - block_lse[..., None])
        value_grad = value_grad + jnp.einsum(
            "hqk,qhc->khc",
            probs.astype(jnp.bfloat16),
            block_grad,
            preferred_element_type=jnp.float32,
        )
        prob_grad = jnp.einsum(
            "qhc,khc->hqk", block_grad, values, preferred_element_type=jnp.float32
        )
        inner = jnp.sum(probs * prob_grad, axis=-1, keepdims=True)
        score_grad = (probs * (prob_grad - inner) * scale).astype(jnp.bfloat16)
        query_grad = jnp.einsum(
            "hqk,khc->qhc", score_grad, keys, preferred_element_type=jnp.float32
        )
        key_grad = key_grad + jnp.einsum(
            "hqk,qhc->khc", score_grad, block, preferred_element_type=jnp.float32
        )
        return ((key_grad, value_grad), query_grad)

    zeros = jnp.zeros((total, heads, width), jnp.float32)
    (key_grad, value_grad), query_grad = lax.scan(
        one_block, (zeros, zeros), (blocks, grad_blocks, logsum)
    )
    return (query_grad.reshape(total, heads, width), key_grad, value_grad)


def layer_forward(x_first, norm_gains, weights):
    w_qkv, w_out, w_up, w_down = weights
    rows_one = spread_rows(layer_norm(x_first, norm_gains[0], norm_gains[1]).astype(jnp.bfloat16))
    total = rows_one.shape[0]
    packed = product_nn(rows_one, w_qkv).astype(jnp.bfloat16).reshape(total, -1, 3, HEAD_DIM)
    attended, logsum = attend(packed[:, :, 0], packed[:, :, 1], packed[:, :, 2])
    x_mid = x_first + fold_rows(product_nn(attended, w_out))
    normed_two = layer_norm(x_mid, norm_gains[2], norm_gains[3]).astype(jnp.bfloat16)
    rows_two = spread_rows(normed_two)
    hidden = product_nn(rows_two, w_up)
    active = jax.nn.gelu(hidden, approximate=False).astype(jnp.bfloat16)
    branch_out = product_nn(active, w_down)
    x_last = x_mid + fold_rows(branch_out)
    return (x_last, (x_first, x_mid, rows_one, rows_two, packed, attended, logsum, hidden))


def norm_back(inputs, gain, bias, grad):
    _, pull = jax.vjp(layer_norm, inputs, gain, bias)
    return pull(grad)


def layer_backward(grad_last, norm_gains, weights, kept):
    w_qkv, w_out, w_up, w_down = weights
    x_first, x_mid, rows_one, rows_two, packed, attended, logsum, hidden = kept
    total = rows_one.shape[0]
    last_low = grad_last.astype(jnp.bfloat16)
    branch_grad = spread_grads(last_low)
    active = jax.nn.gelu(hidden, approximate=False).astype(jnp.bfloat16)
    down_grad = product_tn(active, branch_grad)
    _, gelu_pull = jax.vjp(partial(jax.nn.gelu, approximate=False), hidden)
    hidden_grad = gelu_pull(product_nt(branch_grad, w_down))[0].astype(jnp.bfloat16)
    up_grad = product_tn(rows_two, hidden_grad)
    unit_part = product_nt(hidden_grad, w_up)
    unit_back = fold_grads(unit_part)
    mid_part, gain_grad_two, bias_grad_two = norm_back(
        x_mid, norm_gains[2], norm_gains[3], unit_back
    )
    grad_mid = grad_last + mid_part
    grad_att = spread_grads(grad_mid.astype(jnp.bfloat16))
    out_grad = product_tn(attended, grad_att)
    attended_grad = product_nt(grad_att, w_out).astype(jnp.bfloat16).reshape(total, -1, HEAD_DIM)
    query_grad, key_grad, value_grad = attend_back(
        attended_grad, packed[:, :, 0], packed[:, :, 1], packed[:, :, 2], logsum
    )
    packed_grad = (
        jnp.stack((query_grad, key_grad, value_grad), axis=2)
        .astype(jnp.bfloat16)
        .reshape(total, -1)
    )
    qkv_grad = product_tn(rows_one, packed_grad)
    first_part, gain_grad_one, bias_grad_one = norm_back(
        x_first, norm_gains[0], norm_gains[1], fold_grads(product_nt(packed_grad, w_qkv))
    )
    gain_rows = jnp.stack((gain_grad_one, bias_grad_one, gain_grad_two, bias_grad_two))
    return (grad_mid + first_part, (qkv_grad, out_grad, up_grad, down_grad), gain_rows)


def adam_step(master, grad, first, second, rate):
    first_new = beta_first * first + (1.0 - beta_first) * grad
    second_new = beta_second * second + (1.0 - beta_second) * grad * grad
    update = first_new / first_fix / (jnp.sqrt(second_new / second_fix) + adam_eps)
    return (master - rate * (update + decay_rate * master), first_new, second_new)


def shards(
    fields,
    targets,
    land_mask,
    lead_index,
    var_ids,
    tables,
    norm_gains,
    tables_first,
    tables_second,
    gains_first,
    gains_second,
    w_qkv,
    qkv_first,
    qkv_second,
    w_out,
    out_first,
    out_second,
    w_up,
    up_first,
    up_second,
    w_down,
    down_first,
    down_second,
    qkv_average,
):
    local_samples, shard_rows, _ = fields.shape
    ocean = 1.0 - land_mask.astype(jnp.float32)
    count = lax.psum(jnp.sum(ocean), ("dp", "mp"))
    denom = 2.0 * V * jnp.maximum(count, 1.0)
    var_hot = (var_ids[:, None] == jnp.arange(V, dtype=jnp.int32)[None, :]).astype(jnp.float32)
    first_row = lax.axis_index("mp") * shard_rows
    patch_row = (first_row + jnp.arange(shard_rows, dtype=jnp.int32)) // PATCH_COLS
    row_hot = (patch_row[:, None] == jnp.arange(PATCH_ROWS, dtype=jnp.int32)[None, :]).astype(
        jnp.float32
    )
    lat_rows = jnp.dot(
        row_hot, lat_weights(2 * PATCH_ROWS).reshape(PATCH_ROWS, 2), precision=highest
    )
    lat_pixels = jnp.broadcast_to(lat_rows[:, :, None], (shard_rows, 2, 2)).reshape(shard_rows, 4)
    weights = tuple((master.astype(jnp.bfloat16) for master in (w_qkv, w_out, w_up, w_down)))
    table_grad = jnp.zeros_like(tables)
    gain_grad = jnp.zeros_like(norm_gains)
    matrix_grads = tuple((jnp.zeros(master.shape, jnp.float32) for master in weights))
    loss_part = jnp.float32(0.0)
    inputs = fields[0]
    weighted = jnp.tile(ocean[0] * lat_pixels, (1, V))
    records = []
    for rollout in range(2):
        lead_hot = (jnp.arange(LEADS, dtype=jnp.int32) == lead_index[0, rollout]).astype(
            jnp.float32
        )
        start_rows, embed_pull = jax.vjp(
            lambda cells, table: embed_tokens(cells, table, var_hot, lead_hot), inputs, tables
        )
        last_rows, kept = layer_forward(start_rows, norm_gains, weights)
        guess, head_pull = jax.vjp(predict, last_rows, norm_gains[4], norm_gains[5], tables)
        miss = guess - targets[0, rollout]
        loss_part = loss_part + jnp.sum(weighted * miss * miss)
        records.append((embed_pull, kept, head_pull, 2.0 * weighted * miss / denom))
        inputs = guess
    carried = jnp.zeros_like(inputs)
    for rollout in (1, 0):
        embed_pull, kept, head_pull, loss_grad = records[rollout]
        row_grad, gain_five, gain_six, head_tables = head_pull(loss_grad + carried)
        row_grad, matrix_part, gain_part = layer_backward(row_grad, norm_gains, weights, kept)
        carried, embed_tables = embed_pull(row_grad)
        table_grad = table_grad + head_tables + embed_tables
        gain_grad = gain_grad + jnp.concatenate(
            (gain_part, jnp.stack((gain_five, gain_six))), axis=0
        )
        matrix_grads = tuple((old + new for old, new in zip(matrix_grads, matrix_part)))
    qkv_grad, out_grad, up_grad, down_grad = matrix_grads
    share_rows = D // lax.axis_size("dp")
    dp_index = lax.axis_index("dp")

    def own_share(full, dim):
        return lax.dynamic_slice_in_dim(full, dp_index * share_rows, share_rows, dim)

    summed = lax.psum((qkv_grad, out_grad, up_grad, down_grad), "dp")
    shares = (
        own_share(summed[0], 0),
        own_share(summed[1], 1),
        own_share(summed[2], 0),
        own_share(summed[3], 1),
    )
    table_sum, gain_sum, loss_sum = lax.psum((table_grad, gain_grad, loss_part), ("dp", "mp"))
    share_square = (
        jnp.sum(shares[0] * shares[0])
        + jnp.sum(shares[1] * shares[1])
        + jnp.sum(shares[2] * shares[2])
        + jnp.sum(shares[3] * shares[3])
    )
    square_sum = lax.psum(share_square, ("dp", "mp"))
    grad_norm = jnp.sqrt(square_sum + jnp.sum(table_sum * table_sum) + jnp.sum(gain_sum * gain_sum))
    factor = jnp.minimum(1.0, clip_norm / (grad_norm + 1e-06))
    tab = adam_step(tables, factor * table_sum, tables_first, tables_second, lr_table)
    gai = adam_step(norm_gains, factor * gain_sum, gains_first, gains_second, lr_gain)
    qkv = adam_step(own_share(w_qkv, 0), factor * shares[0], qkv_first, qkv_second, lr_matrix)
    outp = adam_step(own_share(w_out, 1), factor * shares[1], out_first, out_second, lr_matrix)
    upp = adam_step(own_share(w_up, 0), factor * shares[2], up_first, up_second, lr_matrix)
    down = adam_step(own_share(w_down, 1), factor * shares[3], down_first, down_second, lr_matrix)
    average = average_keep * qkv_average + (1.0 - average_keep) * qkv[0]
    return (
        loss_sum / denom,
        grad_norm,
        tab[0],
        tab[1],
        tab[2],
        gai[0],
        gai[1],
        gai[2],
        qkv[0],
        qkv[1],
        qkv[2],
        outp[0],
        outp[1],
        outp[2],
        upp[0],
        upp[1],
        upp[2],
        down[0],
        down[1],
        down[2],
        average,
    )


def solution(mesh):
    return jax.shard_map(
        shards,
        mesh=mesh,
        in_specs=(
            P("dp", "mp", None),
            P("dp", None, "mp", None),
            P("dp", "mp", None),
            P("dp", None),
            P(),
            P(),
            P(),
            P(),
            P(),
            P(),
            P(),
            P(None, "mp"),
            P("dp", "mp"),
            P("dp", "mp"),
            P("mp", None),
            P("mp", "dp"),
            P("mp", "dp"),
            P(None, "mp"),
            P("dp", "mp"),
            P("dp", "mp"),
            P("mp", None),
            P("mp", "dp"),
            P("mp", "dp"),
            P("dp", "mp"),
        ),
        out_specs=(
            P(),
            P(),
            P(),
            P(),
            P(),
            P(),
            P(),
            P(),
            P("dp", "mp"),
            P("dp", "mp"),
            P("dp", "mp"),
            P("mp", "dp"),
            P("mp", "dp"),
            P("mp", "dp"),
            P("dp", "mp"),
            P("dp", "mp"),
            P("dp", "mp"),
            P("mp", "dp"),
            P("mp", "dp"),
            P("mp", "dp"),
            P("dp", "mp"),
        ),
        check_vma=False,
    )
```

profile of v0, /device:TPU:0, one launch (start us, length us, event | category | flops | bytes accessed | tf_op | source)
XLA Modules:
  0.0 1704.5 jit_solution(3737589082572562041)
XLA Ops:
  40.0 46.9 %all-gather.9.cloned.1.call-done = bf16[2048,1024]{1,0:T(8,128)(2,1)} async-done(((bf16[256,1024]{1,0:T(8,128)(2,1)}), bf16[2048,1024]{1,0:T(8,128)(2,1)}) %all-gather.9.cloned.1.call-update) | async-done | bytes 4194320 | tf_op jit(solution)/shard_map/all_gather | solution.py:88
  94.4 23.7 %while.54 = (s32[]{:T(128)}, bf16[4,512,2,64]{1,3,2,0:T(8,128)(2,1)}, f32[4,2,512]{2,1,0:T(2,128)S(1)}, bf16[4,512,2,64]{1,3,2,0:T(8,128)(2,1)S(1)}, bf16[2048,2...) while((s32[]{:T(128)}, bf16[4,512,2,64]{1,3,2,0:T(8,128)(2,1)}, ...), condition=%wide.region_8.9_spmd, body=%wide.region_5.0_spmd.sunk | while | flops 555809792 | bytes 26509408 | solution.py:122
  123.5 48.8 %reduce-scatter.9.cloned.1.call-done = bf16[256,1024]{1,0:T(8,128)(2,1)} async-done(((bf16[2048,1024]{1,0:T(8,128)(2,1)}), bf16[256,1024]{1,0:T(8,128)(2,1)}) %reduce-scatter.9.cloned.1.call-update) | async-done | bytes 524304 | tf_op jit(solution)/shard_map/reduce_scatter | solution.py:92
  181.7 39.4 %all-gather.11.cloned.1.call-done = bf16[2048,1024]{1,0:T(8,128)(2,1)} async-done(((bf16[256,1024]{1,0:T(8,128)(2,1)}), bf16[2048,1024]{1,0:T(8,128)(2,1)}) %all-gather.11.cloned.1.call-update) | async-done | bytes 4194320 | tf_op jit(solution)/shard_map/all_gather | solution.py:88
  242.5 46.5 %reduce-scatter.11.cloned.1.call-done = bf16[256,1024]{1,0:T(8,128)(2,1)} async-done(((bf16[2048,1024]{1,0:T(8,128)(2,1)}), bf16[256,1024]{1,0:T(8,128)(2,1)}) %reduce-scatter.11.cloned.1.call-update) | async-done | bytes 524304 | tf_op jit(solution)/shard_map/reduce_scatter | solution.py:92
  314.3 45.2 %all-gather.13.cloned.1.call-done = bf16[2048,1024]{1,0:T(8,128)(2,1)} async-done(((bf16[256,1024]{1,0:T(8,128)(2,1)}), bf16[2048,1024]{1,0:T(8,128)(2,1)}) %all-gather.13.cloned.1.call-update) | async-done | bytes 4194320 | tf_op jit(solution)/shard_map/all_gather | solution.py:88
  364.5 21.4 %while.55 = (s32[]{:T(128)}, bf16[4,512,2,64]{1,3,2,0:T(8,128)(2,1)S(1)}, f32[4,2,512]{2,1,0:T(2,128)S(1)}, bf16[4,512,2,64]{1,3,2,0:T(8,128)(2,1)S(1)}, bf16[20...) while((s32[]{:T(128)}, bf16[4,512,2,64]{1,3,2,0:T(8,128)(2,1)S(1)}, ...), condition=%wide.region_23.24_spmd, body=%wide.region_20.23_spmd.sunk | while | flops 555809792 | bytes 26509408 | solution.py:122
  390.1 48.8 %reduce-scatter.13.cloned.1.call-done = bf16[256,1024]{1,0:T(8,128)(2,1)} async-done(((bf16[2048,1024]{1,0:T(8,128)(2,1)}), bf16[256,1024]{1,0:T(8,128)(2,1)}) %reduce-scatter.13.cloned.1.call-update) | async-done | bytes 524304 | tf_op jit(solution)/shard_map/reduce_scatter | solution.py:92
  442.5 45.1 %all-gather.15.cloned.1.call-done = bf16[2048,1024]{1,0:T(8,128)(2,1)} async-done(((bf16[256,1024]{1,0:T(8,128)(2,1)}), bf16[2048,1024]{1,0:T(8,128)(2,1)}) %all-gather.15.cloned.1.call-update) | async-done | bytes 4194320 | tf_op jit(solution)/shard_map/all_gather | solution.py:88
  509.1 40.7 %psum.64 = f32[]{:T(128)} all-reduce(f32[]{:T(128)} %fusion.291), channel_id=1, replica_groups=mesh['dp'=4,'mp'=8] {'dp','mp'}, use_global_device_ids=true, to_apply=%region_33.34 | all-reduce | flops 1 | bytes 8 | tf_op jit(solution)/shard_map/psum | solution.py:255
  565.8 44.9 %all-gather.17.cloned.1.call-done = bf16[2048,1024]{1,0:T(8,128)(2,1)} async-done(((bf16[256,1024]{1,0:T(8,128)(2,1)}), bf16[2048,1024]{1,0:T(8,128)(2,1)}) %all-gather.17.cloned.1.call-update) | async-done | bytes 4194320 | tf_op jit(solution)/shard_map/all_gather | solution.py:98
  625.3 48.8 %reduce-scatter.17.cloned.1.call-done = bf16[256,1024]{1,0:T(8,128)(2,1)} async-done(((bf16[2048,1024]{1,0:T(8,128)(2,1)}), bf16[256,1024]{1,0:T(8,128)(2,1)}) %reduce-scatter.17.cloned.1.call-update) | async-done | bytes 524304 | tf_op jit(solution)/shard_map/reduce_scatter | solution.py:102
  679.8 45.3 %all-gather.19.cloned.1.call-done = bf16[2048,1024]{1,0:T(8,128)(2,1)} async-done(((bf16[256,1024]{1,0:T(8,128)(2,1)}), bf16[2048,1024]{1,0:T(8,128)(2,1)}) %all-gather.19.cloned.1.call-update) | async-done | bytes 4194320 | tf_op jit(solution)/shard_map/all_gather | solution.py:98
  733.3 159.9 %while.56 = (s32[]{:T(128)}, f32[2048,2,64]{0,2,1:T(8,128)}, f32[2048,2,64]{0,2,1:T(8,128)S(1)}, bf16[4,512,2,64]{1,3,2,0:T(8,128)(2,1)}, bf16[4,512,2,64]{1,3,2...) while((s32[]{:T(128)}, f32[2048,2,64]{0,2,1:T(8,128)}, ...), condition=%wide.region_41.42_spmd.clone, body=%wide.region_39.41_spmd.clone.sunk | while | flops 1387272192 | bytes 132411568 | solution.py:157
  742.5 15.8 fusion.510
  782.2 15.8 fusion.510
  822.3 15.8 fusion.510
  862.3 15.8 fusion.510
  903.7 47.6 %reduce-scatter.19.cloned.1.call-done = bf16[256,1024]{1,0:T(8,128)(2,1)} async-done(((bf16[2048,1024]{1,0:T(8,128)(2,1)}), bf16[256,1024]{1,0:T(8,128)(2,1)}) %reduce-scatter.19.cloned.1.call-update) | async-done | bytes 524304 | tf_op jit(solution)/shard_map/reduce_scatter | solution.py:102
  993.3 44.9 %all-gather.21.cloned.1.call-done = bf16[2048,1024]{1,0:T(8,128)(2,1)} async-done(((bf16[256,1024]{1,0:T(8,128)(2,1)}), bf16[2048,1024]{1,0:T(8,128)(2,1)}) %all-gather.21.cloned.1.call-update) | async-done | bytes 4194320 | tf_op jit(solution)/shard_map/all_gather | solution.py:98
  1052.7 48.8 %reduce-scatter.21.cloned.1.call-done = bf16[256,1024]{1,0:T(8,128)(2,1)} async-done(((bf16[2048,1024]{1,0:T(8,128)(2,1)}), bf16[256,1024]{1,0:T(8,128)(2,1)}) %reduce-scatter.21.cloned.1.call-update) | async-done | bytes 524304 | tf_op jit(solution)/shard_map/reduce_scatter | solution.py:102
  1107.3 45.2 %all-gather.23.cloned.1.call-done = bf16[2048,1024]{1,0:T(8,128)(2,1)} async-done(((bf16[256,1024]{1,0:T(8,128)(2,1)}), bf16[2048,1024]{1,0:T(8,128)(2,1)}) %all-gather.23.cloned.1.call-update) | async-done | bytes 4194320 | tf_op jit(solution)/shard_map/all_gather | solution.py:98
  1164.3 166.6 %while.57 = (s32[]{:T(128)}, f32[2048,2,64]{0,2,1:T(8,128)}, f32[2048,2,64]{0,2,1:T(8,128)S(1)}, bf16[4,512,2,64]{1,3,2,0:T(8,128)(2,1)}, bf16[4,512,2,64]{1,3,2...) while((s32[]{:T(128)}, f32[2048,2,64]{0,2,1:T(8,128)}, ...), condition=%wide.region_55.56_spmd.clone, body=%wide.region_53.55_spmd.clone.sunk | while | flops 1387272192 | bytes 136605936 | solution.py:157
  1175.2 15.8 fusion.525
  1216.6 15.8 fusion.525
  1232.4 15.1 fusion.523
  1258.4 15.8 fusion.525
  1300.1 15.8 fusion.525
  1315.9 15.1 fusion.523
  1462.4 75.1 %all-reduce.17.cloned.1.call-done = (f32[1024,384]{1,0:T(8,128)}, f32[128,1024]{1,0:T(8,128)}, f32[1024,512]{1,0:T(8,128)}, f32[512,1024]{1,0:T(8,128)}) async-done(((f32[1024,384]{1,0:T(8,128)}, f32[128,1024]{1,0:T(8,128)}, f32[1024,512]{1,0:T(8,128)}, f32[512,1024]{1,0:T(8,128)}), (f32[1024,384]{1,0:T(8,128)}, f32[128,1024]{1,0:T(8,128)}, f32[1024,512]{1,0:T(8,128)}, ...) | async-done | bytes 6291472 | tf_op jit(solution)/shard_map/psum | solution.py:306
  1547.1 40.0 %all-reduce.10 = (f32[]{:T(128)}, f32[]{:T(128)}, f32[6,1024]{1,0:T(8,128)S(1)}) all-reduce(f32[]{:T(128)S(6)} %add.516, f32[]{:T(128)S(6)} %add.528, f32[6,1024]{1,0:T(8,128)S(1)} %add.534), channel_id=1, replica_groups=mesh['dp'=4,'mp'=8] {'dp','mp'}, use_global_device_ids=true, to_apply=%region_31.32 | all-reduce | flops 6146 | bytes 49168 | tf_op jit(solution)/shard_map/psum | solution.py:313
  1588.3 88.0 %all-reduce.15.cloned.1.call-done = f32[440,1024]{1,0:T(8,128)} async-done(((f32[440,1024]{1,0:T(8,128)}), f32[440,1024]{1,0:T(8,128)}) %all-reduce.15.cloned.1.call-update) | async-done | bytes 1802256 | tf_op jit(solution)/shard_map/psum | solution.py:313
  (797 shorter events, 629.7 us)
Async XLA Ops:
  7.2 79.7 %all-gather.9.cloned.1.call-start = ((), (), s32[]{:S(2)}) async-start(), calls=%async_computation.8 | async-start | bytes 4718592 | tf_op jit(solution)/shard_map/all_gather | solution.py:88
  13.2 159.1 %copy-start.136 = (f32[1,1024]{1,0:T(1,128)}, f32[1,1024]{1,0:T(1,128)S(1)}, u32[]{:S(2)}) copy-start(f32[1,1024]{1,0:T(1,128)S(1)} %fusion.284) | copy-start | bytes 12292
  14.7 297.5 %copy-start.126 = (f32[1,1024]{1,0:T(1,128)}, f32[1,1024]{1,0:T(1,128)S(1)}, u32[]{:S(2)}) copy-start(f32[1,1024]{1,0:T(1,128)S(1)} %get-tuple-element.512) | copy-start | bytes 12292
  14.7 549.0 %copy-start.124 = (f32[1,1024]{1,0:T(1,128)}, f32[1,1024]{1,0:T(1,128)S(1)}, u32[]{:S(2)}) copy-start(f32[1,1024]{1,0:T(1,128)S(1)} %get-tuple-element.508) | copy-start | bytes 12292
  16.2 291.7 %copy-start.24 = (f32[48,16,64]{2,1,0:T(8,128)}, f32[48,16,64]{2,1,0:T(8,128)S(1)}, u32[]{:S(2)}) copy-start(f32[48,16,64]{2,1,0:T(8,128)S(1)} %reshape.506) | copy-start | bytes 589828
  35.1 137.2 %copy-start.13 = (f32[256,1024]{1,0:T(8,128)}, f32[256,1024]{1,0:T(8,128)S(1)}, u32[]{:S(2)}) copy-start(f32[256,1024]{1,0:T(8,128)S(1)} %copy.168) | copy-start | bytes 3145732
  37.0 135.4 %reduce-scatter.9.cloned.1.call-start = ((), (), s32[]{:S(2)}) async-start(), calls=%async_computation.9 | async-start | bytes 4718592 | tf_op jit(solution)/shard_map/reduce_scatter | solution.py:92
  123.5 97.7 %all-gather.11.cloned.1.call-start = ((), (), s32[]{:S(2)}) async-start(), calls=%async_computation.10 | async-start | bytes 4718592 | tf_op jit(solution)/shard_map/all_gather | solution.py:88
  173.6 115.3 %copy-start.9 = (f32[256,1024]{1,0:T(8,128)}, f32[256,1024]{1,0:T(8,128)S(1)}, u32[]{:S(2)}) copy-start(f32[256,1024]{1,0:T(8,128)S(1)} %get-tuple-element.494) | copy-start | bytes 3145732
  175.7 113.3 %reduce-scatter.11.cloned.1.call-start = ((), (), s32[]{:S(2)}) async-start(), calls=%async_computation.11 | async-start | bytes 4718592 | tf_op jit(solution)/shard_map/reduce_scatter | solution.py:92
  240.0 119.4 %all-gather.13.cloned.1.call-start = ((), (), s32[]{:S(2)}) async-start(), calls=%async_computation.12 | async-start | bytes 4718592 | tf_op jit(solution)/shard_map/all_gather | solution.py:88
  241.8 197.1 %copy-start.138 = (f32[1,1024]{1,0:T(1,128)}, f32[1,1024]{1,0:T(1,128)S(1)}, u32[]{:S(2)}) copy-start(f32[1,1024]{1,0:T(1,128)S(1)} %fusion.282) | copy-start | bytes 12292
  312.2 126.7 %copy-start.15 = (f32[256,1024]{1,0:T(8,128)}, f32[256,1024]{1,0:T(8,128)S(1)}, u32[]{:S(2)}) copy-start(f32[256,1024]{1,0:T(8,128)S(1)} %copy.177) | copy-start | bytes 3145732
  314.1 124.8 %reduce-scatter.13.cloned.1.call-start = ((), (), s32[]{:S(2)}) async-start(), calls=%async_computation.13 | async-start | bytes 4718592 | tf_op jit(solution)/shard_map/reduce_scatter | solution.py:92
  390.0 97.6 %all-gather.15.cloned.1.call-start = ((), (), s32[]{:S(2)}) async-start(), calls=%async_computation.14 | async-start | bytes 4718592 | tf_op jit(solution)/shard_map/all_gather | solution.py:88
  442.2 115.6 %reduce-scatter.15.cloned.1.call-start = ((), (), s32[]{:S(2)}) async-start(), calls=%async_computation.15 | async-start | bytes 4718592 | tf_op jit(solution)/shard_map/reduce_scatter | solution.py:92
  507.9 102.9 %all-gather.17.cloned.1.call-start = ((), (), s32[]{:S(2)}) async-start(), calls=%async_computation.16 | async-start | bytes 4718592 | tf_op jit(solution)/shard_map/all_gather | solution.py:98
  564.1 113.5 %copy-start.37 = (f32[256,1024]{1,0:T(8,128)}, f32[256,1024]{1,0:T(8,128)S(1)}, u32[]{:S(2)}) copy-start(f32[256,1024]{1,0:T(8,128)S(1)} %get-tuple-element.482) | copy-start | bytes 3145732
  565.3 108.8 %reduce-scatter.17.cloned.1.call-start = ((), (), s32[]{:S(2)}) async-start(), calls=%async_computation.17 | async-start | bytes 4718592 | tf_op jit(solution)/shard_map/reduce_scatter | solution.py:102
  625.2 99.9 %all-gather.19.cloned.1.call-start = ((), (), s32[]{:S(2)}) async-start(), calls=%async_computation.18 | async-start | bytes 4718592 | tf_op jit(solution)/shard_map/all_gather | solution.py:98
  679.6 271.7 %reduce-scatter.19.cloned.1.call-start = ((), (), s32[]{:S(2)}) async-start(), calls=%async_computation.19 | async-start | bytes 4718592 | tf_op jit(solution)/shard_map/reduce_scatter | solution.py:102
  902.4 135.8 %all-gather.21.cloned.1.call-start = ((), (), s32[]{:S(2)}) async-start(), calls=%async_computation.20 | async-start | bytes 4718592 | tf_op jit(solution)/shard_map/all_gather | solution.py:98
  990.9 114.2 %copy-start.184 = (f32[256]{0:T(256)}, f32[256]{0:T(256)S(1)}, u32[]{:S(2)}) copy-start(f32[256]{0:T(256)S(1)} %negate_multiply_fusion.4) | copy-start | bytes 3076
  992.8 108.7 %reduce-scatter.21.cloned.1.call-start = ((), (), s32[]{:S(2)}) async-start(), calls=%async_computation.21 | async-start | bytes 4718592 | tf_op jit(solution)/shard_map/reduce_scatter | solution.py:102
  1052.6 99.9 %all-gather.23.cloned.1.call-start = ((), (), s32[]{:S(2)}) async-start(), calls=%async_computation.22 | async-start | bytes 4718592 | tf_op jit(solution)/shard_map/all_gather | solution.py:98
  1107.1 298.1 %reduce-scatter.23.cloned.1.call-start = ((), (), s32[]{:S(2)}) async-start(), calls=%async_computation.23 | async-start | bytes 4718592 | tf_op jit(solution)/shard_map/reduce_scatter | solution.py:102
  1342.1 195.4 %all-reduce.17.cloned.1.call-start = ((), (), s32[]{:S(2)}) async-start(), calls=%async_computation.25 | async-start | bytes 12582912 | tf_op jit(solution)/shard_map/psum | solution.py:306
  1398.7 277.6 %all-reduce.15.cloned.1.call-start = ((), (), s32[]{:S(2)}) async-start(), calls=%async_computation.24 | async-start | bytes 3604480 | tf_op jit(solution)/shard_map/psum | solution.py:313
  1458.1 222.9 %copy-start.111 = (f32[512,256]{1,0:T(8,128)S(1)}, f32[512,256]{1,0:T(8,128)}, u32[]{:S(2)}) copy-start(f32[512,256]{1,0:T(8,128)} %param.53) | copy-start | bytes 1572868
  1460.9 220.1 %copy-start.112 = (f32[512,256]{1,0:T(8,128)S(1)}, f32[512,256]{1,0:T(8,128)}, u32[]{:S(2)}) copy-start(f32[512,256]{1,0:T(8,128)} %param.54) | copy-start | bytes 1572868
  1460.9 222.8 %copy-start.113 = (f32[256,512]{1,0:T(8,128)S(1)}, f32[256,512]{1,0:T(8,128)}, u32[]{:S(2)}) copy-start(f32[256,512]{1,0:T(8,128)} %param.50) | copy-start | bytes 1572868
  1460.9 222.8 %copy-start.114 = (f32[256,512]{1,0:T(8,128)S(1)}, f32[256,512]{1,0:T(8,128)}, u32[]{:S(2)}) copy-start(f32[256,512]{1,0:T(8,128)} %param.51) | copy-start | bytes 1572868
  (209 other events, 2996.2 us)
Sparse Core Ops, SparseCore 0:
  37.1 49.8 all-gather.8
  123.6 48.7 reduce-scatter.8
  175.8 45.2 all-gather.10
  240.2 48.7 reduce-scatter.10
  314.2 45.2 all-gather.12
  390.1 48.7 reduce-scatter.12
  442.3 45.2 all-gather.14
  508.0 49.7 reduce-scatter.14
  565.4 45.2 all-gather.16
  625.3 48.7 reduce-scatter.16
  679.8 45.2 all-gather.18
  902.6 48.7 reduce-scatter.18
  992.9 45.2 all-gather.20
  1052.7 48.7 reduce-scatter.20
  1107.2 45.2 all-gather.22
  1342.2 48.7 reduce-scatter.22
  1398.8 138.6 all-reduce.16
  1543.3 132.9 all-reduce.14
where the time goes:
time: 1710 us; the launch traced here: 1700 us
  waiting for transfers between devices  813 us (48%)
  matrix products  550 us (32%)
  other arithmetic  120 us (7%)
  local copies, waits for them, and re-layouts  109 us (6%)
  blocking collectives  80.7 us (5%)
  between operations  27.3 us (2%)
    all_gather x4, waiting for transfers between devices, spread_grads(): return lax.all_gather(grad_rows, 'mp', axis=0, tiled=True)  180 us
    all_gather x4, waiting for transfers between devices, spread_rows(): return lax.all_gather(normed, 'mp', axis=0, tiled=True)  177 us
    reduce_scatter x4, waiting for transfers between devices, fold_rows(): lax.psum_scatter(partial_sum.astype(jnp.bfloat16), 'mp', scatter_dimensio...  147 us
    reduce_scatter x4, waiting for transfers between devices, fold_grads(): lax.psum_scatter(partial_sum.astype(jnp.bfloat16), 'mp', scatter_dimensio...  145 us
    dot_general x8, matrix products, one_block(): jnp.einsum('hqk,khc->qhc', score_grad, keys, preferred_element_type=jnp.f...  127 us
    dot_general x8, matrix products, one_block(): jnp.einsum('hqk,qhc->khc', score_grad, block, preferred_element_type=jnp....  120 us
    psum x1, waiting for transfers between devices, shards(): lax.psum((table_grad, gain_grad, loss_part), ('dp', 'mp'))  88 us
    psum x1, waiting for transfers between devices, shards(): summed = lax.psum((qkv_grad, out_grad, up_grad, down_grad), 'dp')  75.1 us
  transfers between devices with their start and end apart: 18, of which 17 were waited for; matrix products, arithmetic and copies ran while one was open for 8% of the time, Pallas kernels for 0%

commit v1 on v0

--- a/solution.py
+++ b/solution.py
@@ -310,7 +310,9 @@
         own_share(summed[2], 0),
         own_share(summed[3], 1),
     )
-    table_sum, gain_sum, loss_sum = lax.psum((table_grad, gain_grad, loss_part), ("dp", "mp"))
+    table_sum, gain_sum, loss_sum = lax.psum(
+        lax.psum((table_grad, gain_grad, loss_part), "mp"), "dp"
+    )
     share_square = (
         jnp.sum(shares[0] * shares[0])
         + jnp.sum(shares[1] * shares[1])

time: 1710 us -> 1780 us (1.041)
  blocking collectives: 80.7 us -> 127 us
  waiting for transfers between devices: 813 us -> 832 us
    psum x1, waiting for transfers between devices: 75.1 us -> 128 us  [shards(): summed = lax.psum((qkv_grad, out_grad, up_grad, down_grad), 'dp')]
    psum x1 -> x3, blocking collectives: 40 us -> 86 us  [the longest x1 40.2 us: shards(): square_sum = lax.psum(share_square, ('dp', 'mp'))]
    psum x1, waiting for transfers between devices: 88 us -> 53.8 us  [shards(): lax.psum((table_grad, gain_grad, loss_part), 'mp')]
  transfers between devices with their start and end apart: 18 -> 18, of which waited for: 17 -> 17; matrix products, arithmetic and copies ran while one was open for 8% -> 4% of each run, Pallas kernels for 0% -> 0%
where the time goes in v1:
time: 1780 us; the launch traced here: 1770 us
  waiting for transfers between devices  832 us (47%)
  matrix products  552 us (31%)
  blocking collectives  127 us (7%)
  other arithmetic  120 us (7%)
  local copies, waits for them, and re-layouts  108 us (6%)
  between operations  27.4 us (2%)
    all_gather x4, waiting for transfers between devices, spread_grads(): return lax.all_gather(grad_rows, 'mp', axis=0, tiled=True)  181 us
    all_gather x4, waiting for transfers between devices, spread_rows(): return lax.all_gather(normed, 'mp', axis=0, tiled=True)  177 us
    reduce_scatter x4, waiting for transfers between devices, fold_rows(): lax.psum_scatter(partial_sum.astype(jnp.bfloat16), 'mp', scatter_dimensio...  147 us
    reduce_scatter x4, waiting for transfers between devices, fold_grads(): lax.psum_scatter(partial_sum.astype(jnp.bfloat16), 'mp', scatter_dimensio...  145 us
    psum x1, waiting for transfers between devices, shards(): summed = lax.psum((qkv_grad, out_grad, up_grad, down_grad), 'dp')  128 us
    dot_general x8, matrix products, one_block(): jnp.einsum('hqk,khc->qhc', score_grad, keys, preferred_element_type=jnp.f...  126 us
    dot_general x8, matrix products, one_block(): jnp.einsum('hqk,qhc->khc', score_grad, block, preferred_element_type=jnp....  120 us
    psum x1, waiting for transfers between devices, shards(): lax.psum((table_grad, gain_grad, loss_part), 'mp')  53.8 us
  transfers between devices with their start and end apart: 18, of which 17 were waited for; matrix products, arithmetic and copies ran while one was open for 4% of the time, Pallas kernels for 0%

profile of v1, /device:TPU:0, one launch (start us, length us, event | category | flops | bytes accessed | tf_op | source)
XLA Modules:
  0.0 1769.6 jit_solution(2710956083773016852)
XLA Ops:
  40.4 46.7 %all-gather.9.cloned.1.call-done = bf16[2048,1024]{1,0:T(8,128)(2,1)} async-done(((bf16[256,1024]{1,0:T(8,128)(2,1)}), bf16[2048,1024]{1,0:T(8,128)(2,1)}) %all-gather.9.cloned.1.call-update) | async-done | bytes 4194320 | tf_op jit(solution)/shard_map/all_gather | solution.py:88
  94.5 23.7 %while.54 = (s32[]{:T(128)}, bf16[4,512,2,64]{1,3,2,0:T(8,128)(2,1)}, f32[4,2,512]{2,1,0:T(2,128)S(1)}, bf16[4,512,2,64]{1,3,2,0:T(8,128)(2,1)S(1)}, bf16[2048,2...) while((s32[]{:T(128)}, bf16[4,512,2,64]{1,3,2,0:T(8,128)(2,1)}, ...), condition=%wide.region_8.9_spmd, body=%wide.region_5.0_spmd.sunk | while | flops 555809792 | bytes 26509408 | solution.py:122
  123.6 48.8 %reduce-scatter.9.cloned.1.call-done = bf16[256,1024]{1,0:T(8,128)(2,1)} async-done(((bf16[2048,1024]{1,0:T(8,128)(2,1)}), bf16[256,1024]{1,0:T(8,128)(2,1)}) %reduce-scatter.9.cloned.1.call-update) | async-done | bytes 524304 | tf_op jit(solution)/shard_map/reduce_scatter | solution.py:92
  181.4 39.8 %all-gather.11.cloned.1.call-done = bf16[2048,1024]{1,0:T(8,128)(2,1)} async-done(((bf16[256,1024]{1,0:T(8,128)(2,1)}), bf16[2048,1024]{1,0:T(8,128)(2,1)}) %all-gather.11.cloned.1.call-update) | async-done | bytes 4194320 | tf_op jit(solution)/shard_map/all_gather | solution.py:88
  242.5 46.4 %reduce-scatter.11.cloned.1.call-done = bf16[256,1024]{1,0:T(8,128)(2,1)} async-done(((bf16[2048,1024]{1,0:T(8,128)(2,1)}), bf16[256,1024]{1,0:T(8,128)(2,1)}) %reduce-scatter.11.cloned.1.call-update) | async-done | bytes 524304 | tf_op jit(solution)/shard_map/reduce_scatter | solution.py:92
  314.4 45.2 %all-gather.13.cloned.1.call-done = bf16[2048,1024]{1,0:T(8,128)(2,1)} async-done(((bf16[256,1024]{1,0:T(8,128)(2,1)}), bf16[2048,1024]{1,0:T(8,128)(2,1)}) %all-gather.13.cloned.1.call-update) | async-done | bytes 4194320 | tf_op jit(solution)/shard_map/all_gather | solution.py:88
  364.6 21.4 %while.55 = (s32[]{:T(128)}, bf16[4,512,2,64]{1,3,2,0:T(8,128)(2,1)S(1)}, f32[4,2,512]{2,1,0:T(2,128)S(1)}, bf16[4,512,2,64]{1,3,2,0:T(8,128)(2,1)S(1)}, bf16[20...) while((s32[]{:T(128)}, bf16[4,512,2,64]{1,3,2,0:T(8,128)(2,1)S(1)}, ...), condition=%wide.region_23.24_spmd, body=%wide.region_20.23_spmd.sunk | while | flops 555809792 | bytes 26509408 | solution.py:122
  390.1 48.8 %reduce-scatter.13.cloned.1.call-done = bf16[256,1024]{1,0:T(8,128)(2,1)} async-done(((bf16[2048,1024]{1,0:T(8,128)(2,1)}), bf16[256,1024]{1,0:T(8,128)(2,1)}) %reduce-scatter.13.cloned.1.call-update) | async-done | bytes 524304 | tf_op jit(solution)/shard_map/reduce_scatter | solution.py:92
  442.8 44.9 %all-gather.15.cloned.1.call-done = bf16[2048,1024]{1,0:T(8,128)(2,1)} async-done(((bf16[256,1024]{1,0:T(8,128)(2,1)}), bf16[2048,1024]{1,0:T(8,128)(2,1)}) %all-gather.15.cloned.1.call-update) | async-done | bytes 4194320 | tf_op jit(solution)/shard_map/all_gather | solution.py:88
  509.0 40.7 %psum.86 = f32[]{:T(128)} all-reduce(f32[]{:T(128)} %fusion.291), channel_id=1, replica_groups=mesh['dp'=4,'mp'=8] {'dp','mp'}, use_global_device_ids=true, to_apply=%region_34.35 | all-reduce | flops 1 | bytes 8 | tf_op jit(solution)/shard_map/psum | solution.py:255
  565.3 45.2 %all-gather.17.cloned.1.call-done = bf16[2048,1024]{1,0:T(8,128)(2,1)} async-done(((bf16[256,1024]{1,0:T(8,128)(2,1)}), bf16[2048,1024]{1,0:T(8,128)(2,1)}) %all-gather.17.cloned.1.call-update) | async-done | bytes 4194320 | tf_op jit(solution)/shard_map/all_gather | solution.py:98
  625.1 48.8 %reduce-scatter.17.cloned.1.call-done = bf16[256,1024]{1,0:T(8,128)(2,1)} async-done(((bf16[2048,1024]{1,0:T(8,128)(2,1)}), bf16[256,1024]{1,0:T(8,128)(2,1)}) %reduce-scatter.17.cloned.1.call-update) | async-done | bytes 524304 | tf_op jit(solution)/shard_map/reduce_scatter | solution.py:102
  679.5 45.3 %all-gather.19.cloned.1.call-done = bf16[2048,1024]{1,0:T(8,128)(2,1)} async-done(((bf16[256,1024]{1,0:T(8,128)(2,1)}), bf16[2048,1024]{1,0:T(8,128)(2,1)}) %all-gather.19.cloned.1.call-update) | async-done | bytes 4194320 | tf_op jit(solution)/shard_map/all_gather | solution.py:98
  733.1 159.0 %while.56 = (s32[]{:T(128)}, f32[2048,2,64]{0,2,1:T(8,128)}, f32[2048,2,64]{0,2,1:T(8,128)S(1)}, bf16[4,512,2,64]{1,3,2,0:T(8,128)(2,1)}, bf16[4,512,2,64]{1,3,2...) while((s32[]{:T(128)}, f32[2048,2,64]{0,2,1:T(8,128)}, ...), condition=%wide.region_42.43_spmd.clone, body=%wide.region_40.42_spmd.clone.sunk | while | flops 1387272192 | bytes 132411568 | solution.py:157
  742.2 15.7 fusion.510
  781.8 15.7 fusion.510
  821.6 15.7 fusion.510
  861.4 15.7 fusion.510
  902.6 47.6 %reduce-scatter.19.cloned.1.call-done = bf16[256,1024]{1,0:T(8,128)(2,1)} async-done(((bf16[2048,1024]{1,0:T(8,128)(2,1)}), bf16[256,1024]{1,0:T(8,128)(2,1)}) %reduce-scatter.19.cloned.1.call-update) | async-done | bytes 524304 | tf_op jit(solution)/shard_map/reduce_scatter | solution.py:102
  992.2 45.2 %all-gather.21.cloned.1.call-done = bf16[2048,1024]{1,0:T(8,128)(2,1)} async-done(((bf16[256,1024]{1,0:T(8,128)(2,1)}), bf16[2048,1024]{1,0:T(8,128)(2,1)}) %all-gather.21.cloned.1.call-update) | async-done | bytes 4194320 | tf_op jit(solution)/shard_map/all_gather | solution.py:98
  1051.7 48.8 %reduce-scatter.21.cloned.1.call-done = bf16[256,1024]{1,0:T(8,128)(2,1)} async-done(((bf16[2048,1024]{1,0:T(8,128)(2,1)}), bf16[256,1024]{1,0:T(8,128)(2,1)}) %reduce-scatter.21.cloned.1.call-update) | async-done | bytes 524304 | tf_op jit(solution)/shard_map/reduce_scatter | solution.py:102
  1106.5 45.1 %all-gather.23.cloned.1.call-done = bf16[2048,1024]{1,0:T(8,128)(2,1)} async-done(((bf16[256,1024]{1,0:T(8,128)(2,1)}), bf16[2048,1024]{1,0:T(8,128)(2,1)}) %all-gather.23.cloned.1.call-update) | async-done | bytes 4194320 | tf_op jit(solution)/shard_map/all_gather | solution.py:98
  1163.4 166.3 %while.57 = (s32[]{:T(128)}, f32[2048,2,64]{0,2,1:T(8,128)}, f32[2048,2,64]{0,2,1:T(8,128)S(1)}, bf16[4,512,2,64]{1,3,2,0:T(8,128)(2,1)}, bf16[4,512,2,64]{1,3,2...) while((s32[]{:T(128)}, f32[2048,2,64]{0,2,1:T(8,128)}, ...), condition=%wide.region_56.57_spmd.clone, body=%wide.region_54.56_spmd.clone.sunk | while | flops 1387272192 | bytes 136605936 | solution.py:157
  1174.2 15.8 fusion.525
  1215.5 15.8 fusion.525
  1257.2 15.8 fusion.525
  1298.8 15.8 fusion.525
  1461.5 53.8 %all-reduce.16.cloned.1.call-done = f32[440,1024]{1,0:T(8,128)} async-done(((f32[440,1024]{1,0:T(8,128)}), f32[440,1024]{1,0:T(8,128)}) %all-reduce.16.cloned.1.call-update) | async-done | bytes 1802256 | tf_op jit(solution)/shard_map/psum | solution.py:314
  1517.1 26.9 %all-reduce.10 = (f32[]{:T(128)}, f32[6,1024]{1,0:T(8,128)S(1)}) all-reduce(f32[]{:T(128)S(6)} %add.522, f32[6,1024]{1,0:T(8,128)S(1)} %add.540), channel_id=1, replica_groups=mesh['dp'=4,'mp'=8] {'mp'}, use_global_device_ids=true, to_apply=%region_31.32 | all-reduce | flops 6145 | bytes 49160 | tf_op jit(solution)/shard_map/psum | solution.py:314
  1543.9 18.9 %all-reduce.11 = (f32[]{:T(128)}, f32[6,1024]{1,0:T(8,128)S(1)}) all-reduce(f32[]{:T(128)} %get-tuple-element.445, f32[6,1024]{1,0:T(8,128)S(1)} %get-tuple-element.446), channel_id=1, replica_groups=mesh['dp'=4,'mp'=8] {'dp'}, use_global_device_ids=true, to_apply=%region_32.33 | all-reduce | flops 6145 | bytes 49160 | tf_op jit(solution)/shard_map/psum | solution.py:313
  1564.2 127.7 %all-reduce.18.cloned.1.call-done = (f32[1024,384]{1,0:T(8,128)}, f32[128,1024]{1,0:T(8,128)}, f32[1024,512]{1,0:T(8,128)}, f32[512,1024]{1,0:T(8,128)}, f32[440,1024]{1,0:T(8,128)}) async-done(((f32[1024,384]{1,0:T(8,128)}, f32[128,1024]{1,0:T(8,128)}, f32[1024,512]{1,0:T(8,128)}, f32[512,1024]{1,0:T(8,128)}, f32[440,1024]{1,0:T(8,128)}), (f32[1024,384]{1,0:T(8,128)}, f32[128,1024]{1,0:T(8,128)}, ...) | async-done | bytes 8093712 | tf_op jit(solution)/shard_map/psum | solution.py:306
  1703.9 40.2 %psum.91 = f32[]{:T(128)} all-reduce(f32[]{:T(128)S(6)} %add.534), channel_id=1, replica_groups=mesh['dp'=4,'mp'=8] {'dp','mp'}, use_global_device_ids=true, to_apply=%region_65.66 | all-reduce | flops 1 | bytes 8 | tf_op jit(solution)/shard_map/psum | solution.py:322
  (793 shorter events, 660.6 us)
Async XLA Ops:
  7.2 79.9 %all-gather.9.cloned.1.call-start = ((), (), s32[]{:S(2)}) async-start(), calls=%async_computation.8 | async-start | bytes 4718592 | tf_op jit(solution)/shard_map/all_gather | solution.py:88
  13.3 159.1 %copy-start.133 = (f32[1,1024]{1,0:T(1,128)}, f32[1,1024]{1,0:T(1,128)S(1)}, u32[]{:S(2)}) copy-start(f32[1,1024]{1,0:T(1,128)S(1)} %fusion.284) | copy-start | bytes 12292
  14.8 297.5 %copy-start.122 = (f32[1,1024]{1,0:T(1,128)}, f32[1,1024]{1,0:T(1,128)S(1)}, u32[]{:S(2)}) copy-start(f32[1,1024]{1,0:T(1,128)S(1)} %get-tuple-element.514) | copy-start | bytes 12292
  14.8 548.8 %copy-start.120 = (f32[1,1024]{1,0:T(1,128)}, f32[1,1024]{1,0:T(1,128)S(1)}, u32[]{:S(2)}) copy-start(f32[1,1024]{1,0:T(1,128)S(1)} %get-tuple-element.510) | copy-start | bytes 12292
  16.2 291.6 %copy-start.24 = (f32[48,16,64]{2,1,0:T(8,128)}, f32[48,16,64]{2,1,0:T(8,128)S(1)}, u32[]{:S(2)}) copy-start(f32[48,16,64]{2,1,0:T(8,128)S(1)} %reshape.506) | copy-start | bytes 589828
  35.3 137.2 %copy-start.13 = (f32[256,1024]{1,0:T(8,128)}, f32[256,1024]{1,0:T(8,128)S(1)}, u32[]{:S(2)}) copy-start(f32[256,1024]{1,0:T(8,128)S(1)} %copy.168) | copy-start | bytes 3145732
  37.1 135.3 %reduce-scatter.9.cloned.1.call-start = ((), (), s32[]{:S(2)}) async-start(), calls=%async_computation.9 | async-start | bytes 4718592 | tf_op jit(solution)/shard_map/reduce_scatter | solution.py:92
  123.6 97.7 %all-gather.11.cloned.1.call-start = ((), (), s32[]{:S(2)}) async-start(), calls=%async_computation.10 | async-start | bytes 4718592 | tf_op jit(solution)/shard_map/all_gather | solution.py:88
  173.7 115.2 %copy-start.9 = (f32[256,1024]{1,0:T(8,128)}, f32[256,1024]{1,0:T(8,128)S(1)}, u32[]{:S(2)}) copy-start(f32[256,1024]{1,0:T(8,128)S(1)} %get-tuple-element.496) | copy-start | bytes 3145732
  175.8 113.2 %reduce-scatter.11.cloned.1.call-start = ((), (), s32[]{:S(2)}) async-start(), calls=%async_computation.11 | async-start | bytes 4718592 | tf_op jit(solution)/shard_map/reduce_scatter | solution.py:92
  240.1 119.5 %all-gather.13.cloned.1.call-start = ((), (), s32[]{:S(2)}) async-start(), calls=%async_computation.12 | async-start | bytes 4718592 | tf_op jit(solution)/shard_map/all_gather | solution.py:88
  241.9 197.1 %copy-start.135 = (f32[1,1024]{1,0:T(1,128)}, f32[1,1024]{1,0:T(1,128)S(1)}, u32[]{:S(2)}) copy-start(f32[1,1024]{1,0:T(1,128)S(1)} %fusion.282) | copy-start | bytes 12292
  312.2 126.7 %copy-start.15 = (f32[256,1024]{1,0:T(8,128)}, f32[256,1024]{1,0:T(8,128)S(1)}, u32[]{:S(2)}) copy-start(f32[256,1024]{1,0:T(8,128)S(1)} %copy.177) | copy-start | bytes 3145732
  314.1 124.9 %reduce-scatter.13.cloned.1.call-start = ((), (), s32[]{:S(2)}) async-start(), calls=%async_computation.13 | async-start | bytes 4718592 | tf_op jit(solution)/shard_map/reduce_scatter | solution.py:92
  390.1 97.6 %all-gather.15.cloned.1.call-start = ((), (), s32[]{:S(2)}) async-start(), calls=%async_computation.14 | async-start | bytes 4718592 | tf_op jit(solution)/shard_map/all_gather | solution.py:88
  442.3 115.4 %reduce-scatter.15.cloned.1.call-start = ((), (), s32[]{:S(2)}) async-start(), calls=%async_computation.15 | async-start | bytes 4718592 | tf_op jit(solution)/shard_map/reduce_scatter | solution.py:92
  507.7 102.8 %all-gather.17.cloned.1.call-start = ((), (), s32[]{:S(2)}) async-start(), calls=%async_computation.16 | async-start | bytes 4718592 | tf_op jit(solution)/shard_map/all_gather | solution.py:98
  564.0 113.5 %copy-start.39 = (f32[256,1024]{1,0:T(8,128)}, f32[256,1024]{1,0:T(8,128)S(1)}, u32[]{:S(2)}) copy-start(f32[256,1024]{1,0:T(8,128)S(1)} %get-tuple-element.484) | copy-start | bytes 3145732
  565.1 108.8 %reduce-scatter.17.cloned.1.call-start = ((), (), s32[]{:S(2)}) async-start(), calls=%async_computation.17 | async-start | bytes 4718592 | tf_op jit(solution)/shard_map/reduce_scatter | solution.py:102
  625.0 99.8 %all-gather.19.cloned.1.call-start = ((), (), s32[]{:S(2)}) async-start(), calls=%async_computation.18 | async-start | bytes 4718592 | tf_op jit(solution)/shard_map/all_gather | solution.py:98
  679.4 270.8 %reduce-scatter.19.cloned.1.call-start = ((), (), s32[]{:S(2)}) async-start(), calls=%async_computation.19 | async-start | bytes 4718592 | tf_op jit(solution)/shard_map/reduce_scatter | solution.py:102
  901.3 136.1 %all-gather.21.cloned.1.call-start = ((), (), s32[]{:S(2)}) async-start(), calls=%async_computation.20 | async-start | bytes 4718592 | tf_op jit(solution)/shard_map/all_gather | solution.py:98
  990.0 114.2 %copy-start.182 = (f32[256]{0:T(256)}, f32[256]{0:T(256)S(1)}, u32[]{:S(2)}) copy-start(f32[256]{0:T(256)S(1)} %negate_multiply_fusion.4) | copy-start | bytes 3076
  992.0 108.6 %reduce-scatter.21.cloned.1.call-start = ((), (), s32[]{:S(2)}) async-start(), calls=%async_computation.21 | async-start | bytes 4718592 | tf_op jit(solution)/shard_map/reduce_scatter | solution.py:102
  1051.7 99.9 %all-gather.23.cloned.1.call-start = ((), (), s32[]{:S(2)}) async-start(), calls=%async_computation.22 | async-start | bytes 4718592 | tf_op jit(solution)/shard_map/all_gather | solution.py:98
  1106.2 291.4 %reduce-scatter.23.cloned.1.call-start = ((), (), s32[]{:S(2)}) async-start(), calls=%async_computation.23 | async-start | bytes 4718592 | tf_op jit(solution)/shard_map/reduce_scatter | solution.py:102
  1340.8 174.5 %all-reduce.16.cloned.1.call-start = ((), (), s32[]{:S(2)}) async-start(), calls=%async_computation.24 | async-start | bytes 3604480 | tf_op jit(solution)/shard_map/psum | solution.py:314
  1453.2 238.7 %all-reduce.18.cloned.1.call-start = ((), (), s32[]{:S(2)}) async-start(), calls=%async_computation.25 | async-start | bytes 16187392 | tf_op jit(solution)/shard_map/psum | solution.py:306
  1515.3 230.8 %copy-start.109 = (f32[512,256]{1,0:T(8,128)S(1)}, f32[512,256]{1,0:T(8,128)}, u32[]{:S(2)}) copy-start(f32[512,256]{1,0:T(8,128)} %param.53) | copy-start | bytes 1572868
  1515.3 230.8 %copy-start.110 = (f32[512,256]{1,0:T(8,128)S(1)}, f32[512,256]{1,0:T(8,128)}, u32[]{:S(2)}) copy-start(f32[512,256]{1,0:T(8,128)} %param.54) | copy-start | bytes 1572868
  1515.3 233.6 %copy-start.111 = (f32[256,512]{1,0:T(8,128)S(1)}, f32[256,512]{1,0:T(8,128)}, u32[]{:S(2)}) copy-start(f32[256,512]{1,0:T(8,128)} %param.50) | copy-start | bytes 1572868
  1515.3 233.6 %copy-start.112 = (f32[256,512]{1,0:T(8,128)S(1)}, f32[256,512]{1,0:T(8,128)}, u32[]{:S(2)}) copy-start(f32[256,512]{1,0:T(8,128)} %param.51) | copy-start | bytes 1572868
  (206 other events, 3194.6 us)
Sparse Core Ops, SparseCore 0:
  37.2 49.8 all-gather.8
  123.7 48.7 reduce-scatter.8
  175.9 45.2 all-gather.10
  240.2 48.7 reduce-scatter.10
  314.2 45.2 all-gather.12
  390.2 48.7 reduce-scatter.12
  442.4 45.2 all-gather.14
  507.9 49.7 reduce-scatter.14
  565.2 45.3 all-gather.16
  625.2 48.7 reduce-scatter.16
  679.5 45.2 all-gather.18
  901.5 48.7 reduce-scatter.18
  992.1 45.2 all-gather.20
  1051.8 48.7 reduce-scatter.20
  1106.3 45.2 all-gather.22
  1340.9 48.7 reduce-scatter.22
  1453.3 61.9 all-reduce.15
  1520.8 171.0 all-reduce.17
